TPU v7x, 32 devices: a whole 2x2x4 slice. The times are simulated.
32 devices in a mesh: row: 4 (over y, x), col: 8 (over z, core).
Axes of the slice: x: 2, y: 2, z: 4, core: 2. Of those that a mesh axis runs over, the one named last changes fastest.
Arguments:
- features: float32 [2048, 256], P(('row', 'col')), may hold values from -6 to 6
- tile_vals: float32 [4, 8, 4, 128, 128], P('row', 'col'), may hold values from -0.1875 to 0.1875
- tile_ids: int32 [4, 8, 4], P('row', 'col'), may hold values from 0 to 7, as said below
- tile_count: int32 [4, 8], P('row', 'col'), may hold values from 2 to 4, as said below
- weight: float32 [256, 256], replicated, may hold values from -0.375 to 0.375
Outputs:
- activations: float32 [8, 256, 256], P('col', 'row')
Inputs may be any that keep to these rules, and one draw needn't show every extreme that they name: `tile_ids`: the first tile_count entries of a region's list name distinct tiles; later entries are unused. `tile_count`: some region lists 4 tiles in every draw.
All inputs are finite; a program needn't handle non-finite values.
Results may differ from a plain program's by a relative error of at most 0.0003.
Values sent between devices are 32-bit elements; how exact they have to be, the bound alone decides.
A program may use at most 64 MiB of HBM per device.

v0:
```python
import functools

import jax
import jax.numpy as jnp
from jax import lax
from jax.experimental import pallas as pl
from jax.experimental.pallas import tpu as pltpu
from jax.sharding import PartitionSpec as P

LANES = 256
MESH = pl.DeviceIdType.MESH


def split(x):
    high = x.astype(jnp.bfloat16)
    low = (x - high.astype(jnp.float32)).astype(jnp.bfloat16)
    return high, low


def dot3(a_high, a_low, b_high, b_low):
    mul = functools.partial(jnp.dot, preferred_element_type=jnp.float32)
    return mul(a_high, b_high) + (mul(a_low, b_high) + mul(a_high, b_low))


def loop(count, body):
    if count <= 8:
        for i in range(count):
            body(i)
    else:
        lax.fori_loop(0, count, lambda i, c: (body(i), c)[1], 0)


def kernel(
    rows, cols,
    feat_ref, vals_ref, ids_hbm, count_hbm, weight_ref, out_ref, ids_ref, count_ref,
    xbuf, vals, weight, adj, wsplit, part, landed,
    local_sem, send_own, send_par, send_rel, recv_ring, recv_par, send_rs, recv_rs, ready,
):
    me_row, me_col = lax.axis_index("row"), lax.axis_index("col")
    chips = cols // 2
    chip, core = me_col // 2, me_col % 2
    piece = feat_ref.shape[0]
    chunks = feat_ref.shape[1] // LANES
    slots, tile = vals.shape[0], vals.shape[1]
    col_tiles = cols * piece // tile
    row_tiles = rows * piece // tile
    upward = [d for d in (1, 2) if d < chips]
    downward = list(range(1 - chips, 0))

    def inside(d):
        return jnp.logical_and(chip + d >= 0, chip + d < chips)

    load_own = [
        pltpu.make_async_copy(
            feat_ref.at[:, pl.ds(h * LANES, LANES)], xbuf.at[h, me_col], local_sem.at[2 + h]
        )
        for h in range(chunks)
    ]
    load_vals = pltpu.make_async_copy(vals_ref.at[0, 0], vals, local_sem.at[0])
    load_weight = pltpu.make_async_copy(weight_ref, weight, local_sem.at[1])
    load_ids = pltpu.make_async_copy(ids_hbm, ids_ref, local_sem.at[2 + chunks])
    load_count = pltpu.make_async_copy(count_hbm, count_ref, local_sem.at[3 + chunks])
    load_ids.start()
    load_count.start()
    load_vals.start()
    load_weight.start()
    for copy in load_own:
        copy.start()

    barrier = pltpu.get_barrier_semaphore()
    expected = jnp.int32(rows)
    for s in range(1, rows):
        pl.semaphore_signal(
            barrier, inc=1, device_id=(lax.rem(me_row + s, rows), me_col), device_id_type=MESH
        )
    pl.semaphore_signal(barrier, inc=1, device_id=(me_row, chip * 2 + 1 - core), device_id_type=MESH)
    for d in range(1, chips):
        expected = expected + inside(-d).astype(jnp.int32)

        @pl.when(inside(d))
        def _(d=d):
            pl.semaphore_signal(barrier, inc=1, device_id=(me_row, me_col + 2 * d), device_id_type=MESH)

    for h in range(chunks):
        load_own[h].wait()
    pl.semaphore_wait(barrier, expected)

    def own_send(h, n, d):
        return pltpu.make_async_remote_copy(
            src_ref=xbuf.at[h, me_col], dst_ref=xbuf.at[h, me_col],
            send_sem=send_own.at[h, n], recv_sem=recv_ring.at[h, chip],
            device_id=(me_row, me_col + 2 * d), device_id_type=MESH,
        )

    def partner_own(h):
        return pltpu.make_async_remote_copy(
            src_ref=xbuf.at[h, me_col], dst_ref=xbuf.at[h, me_col],
            send_sem=send_par.at[h, chip], recv_sem=recv_par.at[h, chip],
            device_id=(me_row, chip * 2 + 1 - core), device_id_type=MESH,
        )

    def partner_pass(h, p):
        return pltpu.make_async_remote_copy(
            src_ref=xbuf.at[h, 2 * p + core], dst_ref=xbuf.at[h, 2 * p + core],
            send_sem=send_par.at[h, p], recv_sem=recv_par.at[h, p],
            device_id=(me_row, chip * 2 + 1 - core), device_id_type=MESH,
        )

    def relay(h, p, step):
        return pltpu.make_async_remote_copy(
            src_ref=xbuf.at[h, 2 * p + core], dst_ref=xbuf.at[h, 2 * p + core],
            send_sem=send_rel.at[h, p], recv_sem=recv_ring.at[h, p],
            device_id=(me_row, me_col + 2 * step), device_id_type=MESH,
        )

    def from_partner(h, p):
        return pltpu.make_async_remote_copy(
            src_ref=xbuf.at[h, 2 * p + 1 - core], dst_ref=xbuf.at[h, 2 * p + 1 - core],
            send_sem=send_par.at[h, p], recv_sem=recv_par.at[h, p],
            device_id=(me_row, chip * 2 + 1 - core), device_id_type=MESH,
        )

    def scatter(h, s):
        owner = lax.rem(me_row + s, rows)
        return pltpu.make_async_remote_copy(
            src_ref=part.at[h, pl.ds(owner * piece, piece)], dst_ref=landed.at[h, s - 1],
            send_sem=send_rs.at[h, s - 1], recv_sem=recv_rs.at[h, s - 1],
            device_id=(owner, me_col), device_id_type=MESH,
        )

    for n, d in enumerate(upward):

        @pl.when(inside(-d))
        def _(n=n, d=d):
            pl.semaphore_signal(
                ready.at[n], inc=1, device_id=(me_row, me_col - 2 * d), device_id_type=MESH
            )

    for n, d in enumerate(downward):
        for h in range(chunks):
            pl.when(inside(d))(own_send(h, len(upward) + n, d).start)
    for h in range(chunks):
        partner_own(h).start()

    def send_up(n, d):
        @pl.when(inside(d))
        def _():
            pl.semaphore_wait(ready.at[n], 1)
            for h in range(chunks):
                own_send(h, n, d).start()

    for n, d in enumerate(upward[:1]):
        send_up(n, d)
    load_ids.wait()
    load_count.wait()
    load_vals.wait()

    def place(t):
        found = jnp.int32(0)
        slot = jnp.int32(0)

        def look(k, carry):
            hit = jnp.logical_and(ids_ref[0, 0, k] == t, k < count_ref[0, 0])
            return jnp.where(hit, 1, carry[0]), jnp.where(hit, k, carry[1])

        found, slot = lax.fori_loop(0, slots, look, (found, slot), unroll=slots <= 8)
        high, low = split(jnp.where(found == 1, vals[slot], 0.0))
        at = (pl.ds((t // col_tiles) * tile, tile), pl.ds((t % col_tiles) * tile, tile))
        adj[(0,) + at] = high
        adj[(1,) + at] = low

    loop(row_tiles * col_tiles, place)

    load_weight.wait()
    high, low = split(weight[...])
    wsplit[0] = high
    wsplit[1] = low

    for n, d in enumerate(upward[1:], 1):
        send_up(n, d)

    block = min(256, rows * piece)
    for h in range(chunks):
        for step in (1, -1):
            for d in range(1, chips):
                p = chip - step * d

                @pl.when(inside(-step * d))
                def _(h=h, d=d, step=step, p=p):
                    relay(h, p, step).wait_recv()
                    if d >= 2 and step == 1:
                        pl.when(inside(step))(relay(h, p, step).start)
                    partner_pass(h, p).start()

        for p in range(chips):
            from_partner(h, p).wait_recv()

        x_high, x_low = split(xbuf[h].reshape(cols * piece, LANES))

        def product(b):
            at = pl.ds(b * block, block)
            part[h, at, :] = dot3(adj[0, at, :], adj[1, at, :], x_high, x_low)

        loop(rows * piece // block, product)
        for s in range(1, rows):
            scatter(h, s).start()

    mixed = jnp.zeros((piece, weight.shape[1]), jnp.float32)
    for h in range(chunks):
        owned = part[h, pl.ds(me_row * piece, piece), :]
        for s in range(1, rows):
            scatter(h, s).wait_recv()
            owned = owned + landed[h, s - 1]
        o_high, o_low = split(owned)
        at = pl.ds(h * LANES, LANES)
        mixed = mixed + dot3(o_high, o_low, wsplit[0, at, :], wsplit[1, at, :])
    out_ref[...] = jnp.maximum(mixed, 0.0)

    for h in range(chunks):
        for n, d in enumerate(upward + downward):
            pl.when(inside(d))(own_send(h, n, d).wait_send)
        partner_own(h).wait_send()
        for d in range(1, chips):
            for step in (1, -1):
                p = chip - step * d

                @pl.when(inside(-step * d))
                def _(h=h, d=d, step=step, p=p):
                    partner_pass(h, p).wait_send()
                    if d >= 2 and step == 1:
                        pl.when(inside(step))(relay(h, p, step).wait_send)

        for s in range(1, rows):
            scatter(h, s).wait_send()


def local(rows, cols, features, tile_vals, tile_ids, tile_count, weight):
    piece, width = features.shape
    chunks = width // LANES
    chips = cols // 2
    slots, tile = tile_vals.shape[2], tile_vals.shape[3]
    f32, bf16 = jnp.float32, jnp.bfloat16
    dma = pltpu.SemaphoreType.DMA
    out = pl.pallas_call(
        functools.partial(kernel, rows, cols),
        out_shape=jax.ShapeDtypeStruct((piece, weight.shape[1]), f32),
        in_specs=[
            pl.BlockSpec(memory_space=pl.ANY),
            pl.BlockSpec(memory_space=pl.ANY),
            pl.BlockSpec(memory_space=pl.ANY),
            pl.BlockSpec(memory_space=pl.ANY),
            pl.BlockSpec(memory_space=pl.ANY),
        ],
        out_specs=pl.BlockSpec(memory_space=pltpu.VMEM),
        scratch_shapes=[
            pltpu.SMEM(tile_ids.shape, jnp.int32),
            pltpu.SMEM(tile_count.shape, jnp.int32),
            pltpu.VMEM((chunks, cols, piece, LANES), f32),
            pltpu.VMEM((slots, tile, tile), f32),
            pltpu.VMEM(weight.shape, f32),
            pltpu.VMEM((2, rows * piece, cols * piece), bf16),
            pltpu.VMEM((2,) + weight.shape, bf16),
            pltpu.VMEM((chunks, rows * piece, LANES), f32),
            pltpu.VMEM((chunks, rows - 1, piece, LANES), f32),
            dma((4 + chunks,)),
            dma((chunks, 2 + chips)),
            dma((chunks, chips)),
            dma((chunks, chips)),
            dma((chunks, chips)),
            dma((chunks, chips)),
            dma((chunks, rows - 1)),
            dma((chunks, rows - 1)),
            pltpu.SemaphoreType.REGULAR((2,)),
        ],
        compiler_params=pltpu.CompilerParams(collective_id=0, has_side_effects=True),
    )(features, tile_vals, tile_ids, tile_count, weight)
    return out.reshape(1, piece, weight.shape[1])


def solution(mesh):
    in_specs = (
        P(("row", "col"), None),
        P("row", "col", None, None, None),
        P("row", "col", None),
        P("row", "col"),
        P(),
    )
    body = functools.partial(local, mesh.shape["row"], mesh.shape["col"])
    return jax.shard_map(
        body, mesh=mesh, in_specs=in_specs, out_specs=P("col", "row", None), check_vma=False
    )
```

profile of v0, /device:TPU:0, one launch (start us, length us, event | category | flops | bytes accessed | tf_op | source)
XLA Modules:
  0.0 19.9 jit_solution(10162174603462883710)
XLA Ops:
  0.7 17.8 %shard_map.55 = f32[64,256]{1,0:T(8,128)} custom-call(f32[64,256]{1,0:T(8,128)} %feat_ref.1, f32[1,1,4,128,128]{4,3,2,1,0:T(8,128)} %vals_ref.1, s32[1,1,4]{2,1,0:T(1,128)} %ids_hbm.1, s32[1,1]{1,0:T(1,128)S(6)} %copy.7.count_hbm, f32[256,256]{1,0:T(8,128)} %weight_ref.1), custom_call_target="tpu_custom_call" | custom-call | tf_op jit(solution)/shard_map/pallas_call | solution.py:244
  18.4 1.5 %copy.8 = f32[1,64,256]{2,1,0:T(8,128)} copy(f32[1,64,256]{2,1,0:T(8,128)} %bitcast.1) | data formatting | bytes 131072
where the time goes:
time: 20.1 us; the launch traced here: 19.9 us
  Pallas kernels  17.8 us (89%)
  local copies, waits for them, and re-layouts  1.47 us (7%)
  between operations  0.66 us (3%)
    pallas_call x1, Pallas kernels, local(): pl.pallas_call(functools.partial(kernel, rows, cols), out_shape=jax.Shape...  17.8 us
    unnamed x1, local copies, waits for them, and re-layouts  1.47 us

commit v1 on v0

--- a/solution.py
+++ b/solution.py
@@ -20,6 +20,15 @@
 def dot3(a_high, a_low, b_high, b_low):
     mul = functools.partial(jnp.dot, preferred_element_type=jnp.float32)
     return mul(a_high, b_high) + (mul(a_low, b_high) + mul(a_high, b_low))
+
+
+def flip(index, bits):
+    bit = 1
+    while bit <= bits:
+        if bits & bit:
+            index = index + bit * (1 - 2 * (index // bit % 2))
+        bit *= 2
+    return index
 
 
 def loop(count, body):
@@ -81,20 +90,21 @@
         def _(d=d):
             pl.semaphore_signal(barrier, inc=1, device_id=(me_row, me_col + 2 * d), device_id_type=MESH)
 
-    for h in range(chunks):
-        load_own[h].wait()
     pl.semaphore_wait(barrier, expected)
 
+    def own(h):
+        return feat_ref.at[:, pl.ds(h * LANES, LANES)]
+
     def own_send(h, n, d):
         return pltpu.make_async_remote_copy(
-            src_ref=xbuf.at[h, me_col], dst_ref=xbuf.at[h, me_col],
+            src_ref=own(h), dst_ref=xbuf.at[h, me_col],
             send_sem=send_own.at[h, n], recv_sem=recv_ring.at[h, chip],
             device_id=(me_row, me_col + 2 * d), device_id_type=MESH,
         )
 
     def partner_own(h):
         return pltpu.make_async_remote_copy(
-            src_ref=xbuf.at[h, me_col], dst_ref=xbuf.at[h, me_col],
+            src_ref=own(h), dst_ref=xbuf.at[h, me_col],
             send_sem=send_par.at[h, chip], recv_sem=recv_par.at[h, chip],
             device_id=(me_row, chip * 2 + 1 - core), device_id_type=MESH,
         )
@@ -121,7 +131,7 @@
         )
 
     def scatter(h, s):
-        owner = lax.rem(me_row + s, rows)
+        owner = flip(me_row, s)
         return pltpu.make_async_remote_copy(
             src_ref=part.at[h, pl.ds(owner * piece, piece)], dst_ref=landed.at[h, s - 1],
             send_sem=send_rs.at[h, s - 1], recv_sem=recv_rs.at[h, s - 1],
@@ -192,6 +202,7 @@
                         pl.when(inside(step))(relay(h, p, step).start)
                     partner_pass(h, p).start()
 
+        load_own[h].wait()
         for p in range(chips):
             from_partner(h, p).wait_recv()
 
@@ -202,7 +213,7 @@
             part[h, at, :] = dot3(adj[0, at, :], adj[1, at, :], x_high, x_low)
 
         loop(rows * piece // block, product)
-        for s in range(1, rows):
+        for s in reversed(range(1, rows)):
             scatter(h, s).start()
 
     mixed = jnp.zeros((piece, weight.shape[1]), jnp.float32)
@@ -243,7 +254,7 @@
     dma = pltpu.SemaphoreType.DMA
     out = pl.pallas_call(
         functools.partial(kernel, rows, cols),
-        out_shape=jax.ShapeDtypeStruct((piece, weight.shape[1]), f32),
+        out_shape=pltpu.VMEM((piece, weight.shape[1]), f32),
         in_specs=[
             pl.BlockSpec(memory_space=pl.ANY),
             pl.BlockSpec(memory_space=pl.ANY),

time: 20.1 us -> 18.9 us (0.940)
  local copies, waits for them, and re-layouts: 1.47 us -> 0.63 us
  Pallas kernels: 17.8 us -> 17.4 us
    unnamed x1, local copies, waits for them, and re-layouts: 1.47 us -> 0.63 us
    pallas_call x1, Pallas kernels: 17.8 us -> 17.4 us  [local(): pl.pallas_call(functools.partial(kernel, rows, cols), out_shape=pltpu.VME...]
where the time goes in v1:
time: 18.9 us; the launch traced here: 18.7 us
  Pallas kernels  17.4 us (92%)
  between operations  0.66 us (3%)
  local copies, waits for them, and re-layouts  0.63 us (3%)
    pallas_call x1, Pallas kernels, local(): pl.pallas_call(functools.partial(kernel, rows, cols), out_shape=pltpu.VME...  17.4 us
    unnamed x1, local copies, waits for them, and re-layouts  0.63 us

profile of v1, /device:TPU:0, one launch (start us, length us, event | category | flops | bytes accessed | tf_op | source)
XLA Modules:
  0.0 18.7 jit_solution(15530115075185496222)
XLA Ops:
  0.7 17.4 %shard_map.55 = f32[64,256]{1,0:T(8,128)S(1)} custom-call(f32[64,256]{1,0:T(8,128)} %feat_ref.1, f32[1,1,4,128,128]{4,3,2,1,0:T(8,128)} %vals_ref.1, s32[1,1,4]{2,1,0:T(1,128)} %ids_hbm.1, s32[1,1]{1,0:T(1,128)S(6)} %copy.8.count_hbm, f32[256,256]{1,0:T(8,128)} %weight_ref.1), custom_call_target="tpu_custom_call" | custom-call | tf_op jit(solution)/shard_map/pallas_call | solution.py:255
  18.1 0.6 %copy.7 = f32[1,64,256]{2,1,0:T(8,128)} copy(f32[1,64,256]{2,1,0:T(8,128)S(1)} %bitcast.1) | data formatting | bytes 131072

commit v2 on v1

--- a/solution.py
+++ b/solution.py
@@ -43,7 +43,7 @@
     rows, cols,
     feat_ref, vals_ref, ids_hbm, count_hbm, weight_ref, out_ref, ids_ref, count_ref,
     xbuf, vals, weight, adj, wsplit, part, landed,
-    local_sem, send_own, send_par, send_rel, recv_ring, recv_par, send_rs, recv_rs, ready,
+    local_sem, send_own, send_par, send_rel, recv_ring, recv_par, send_rs, recv_rs, ready, ready_row, ready_par,
 ):
     me_row, me_col = lax.axis_index("row"), lax.axis_index("col")
     chips = cols // 2
@@ -77,12 +77,18 @@
         copy.start()
 
     barrier = pltpu.get_barrier_semaphore()
-    expected = jnp.int32(rows)
+    partner = chip * 2 + 1 - core
+    expected = me_row + core
     for s in range(1, rows):
-        pl.semaphore_signal(
-            barrier, inc=1, device_id=(lax.rem(me_row + s, rows), me_col), device_id_type=MESH
-        )
-    pl.semaphore_signal(barrier, inc=1, device_id=(me_row, chip * 2 + 1 - core), device_id_type=MESH)
+
+        @pl.when(me_row + s < rows)
+        def _(s=s):
+            pl.semaphore_signal(barrier, inc=1, device_id=(me_row + s, me_col), device_id_type=MESH)
+
+    @pl.when(core == 0)
+    def _():
+        pl.semaphore_signal(barrier, inc=1, device_id=(me_row, partner), device_id_type=MESH)
+
     for d in range(1, chips):
         expected = expected + inside(-d).astype(jnp.int32)
 
@@ -90,7 +96,9 @@
         def _(d=d):
             pl.semaphore_signal(barrier, inc=1, device_id=(me_row, me_col + 2 * d), device_id_type=MESH)
 
-    pl.semaphore_wait(barrier, expected)
+    @pl.when(expected > 0)
+    def _():
+        pl.semaphore_wait(barrier, expected)
 
     def own(h):
         return feat_ref.at[:, pl.ds(h * LANES, LANES)]
@@ -149,6 +157,23 @@
     for n, d in enumerate(downward):
         for h in range(chunks):
             pl.when(inside(d))(own_send(h, len(upward) + n, d).start)
+
+    @pl.when(core == 1)
+    def _():
+        pl.semaphore_signal(ready_par, inc=1, device_id=(me_row, partner), device_id_type=MESH)
+
+    for s in range(1, rows):
+
+        @pl.when(flip(me_row, s) < me_row)
+        def _(s=s):
+            pl.semaphore_signal(
+                ready_row.at[s - 1], inc=1, device_id=(flip(me_row, s), me_col), device_id_type=MESH
+            )
+
+    @pl.when(core == 0)
+    def _():
+        pl.semaphore_wait(ready_par, 1)
+
     for h in range(chunks):
         partner_own(h).start()
 
@@ -214,6 +239,12 @@
 
         loop(rows * piece // block, product)
         for s in reversed(range(1, rows)):
+            if h == 0:
+
+                @pl.when(flip(me_row, s) > me_row)
+                def _(s=s):
+                    pl.semaphore_wait(ready_row.at[s - 1], 1)
+
             scatter(h, s).start()
 
     mixed = jnp.zeros((piece, weight.shape[1]), jnp.float32)
@@ -282,6 +313,8 @@
             dma((chunks, rows - 1)),
             dma((chunks, rows - 1)),
             pltpu.SemaphoreType.REGULAR((2,)),
+            pltpu.SemaphoreType.REGULAR((rows - 1,)),
+            pltpu.SemaphoreType.REGULAR,
         ],
         compiler_params=pltpu.CompilerParams(collective_id=0, has_side_effects=True),
     )(features, tile_vals, tile_ids, tile_count, weight)

time: 18.9 us -> 18.8 us (level)
  Pallas kernels: 17.4 us -> 17.2 us
    pallas_call x1, Pallas kernels: 17.4 us -> 17.2 us  [local(): pl.pallas_call(functools.partial(kernel, rows, cols), out_shape=pltpu.VME...]
where the time goes in v2:
time: 18.8 us; the launch traced here: 18.5 us
  Pallas kernels  17.2 us (91%)
  between operations  0.66 us (4%)
  local copies, waits for them, and re-layouts  0.63 us (3%)
    pallas_call x1, Pallas kernels, local(): pl.pallas_call(functools.partial(kernel, rows, cols), out_shape=pltpu.VME...  17.2 us
    unnamed x1, local copies, waits for them, and re-layouts  0.63 us

profile of v2, /device:TPU:0, one launch (start us, length us, event | category | flops | bytes accessed | tf_op | source)
XLA Modules:
  0.0 18.5 jit_solution(12056862965496881779)
XLA Ops:
  0.7 17.2 %shard_map.55 = f32[64,256]{1,0:T(8,128)S(1)} custom-call(f32[64,256]{1,0:T(8,128)} %feat_ref.1, f32[1,1,4,128,128]{4,3,2,1,0:T(8,128)} %vals_ref.1, s32[1,1,4]{2,1,0:T(1,128)} %ids_hbm.1, s32[1,1]{1,0:T(1,128)S(6)} %copy.8.count_hbm, f32[256,256]{1,0:T(8,128)} %weight_ref.1), custom_call_target="tpu_custom_call" | custom-call | tf_op jit(solution)/shard_map/pallas_call | solution.py:286
  17.9 0.6 %copy.7 = f32[1,64,256]{2,1,0:T(8,128)} copy(f32[1,64,256]{2,1,0:T(8,128)S(1)} %bitcast.1) | data formatting | bytes 131072
